TPU v7x, 32 devices: a whole 2x2x4 slice. The times are simulated.
32 devices in a mesh: section: 4 (over y, core), dp: 8 (over z, x).
Axes of the slice: x: 2, y: 2, z: 4, core: 2. Of those that a mesh axis runs over, the one named last changes fastest.
Arguments:
- patches: bfloat16 [16, 197, 768], P('dp'), may hold values from -6 to 6
- page_mask: int32 [16, 197], P('dp'), may hold values from 0 to 1, as said below
- mask_token: bfloat16 [768], replicated, may hold values from -6 to 6
- buckets: int32 [197, 197], replicated, may hold values from 0 to 731
- ln_gain: bfloat16 [4, 768], P('section'), may hold values from 0.25 to 1.75
- ln_shift: bfloat16 [4, 768], P('section'), may hold values from -4 to 4
- layer_scale: bfloat16 [4, 768], P('section'), may hold values from 0.25 to 1.75
- branch_bias: bfloat16 [4, 768], P('section'), may hold values from -4 to 4
- qkv_weight: bfloat16 [2, 768, 2304], P(None, 'dp'), may hold values from -0.21875 to 0.21875
- qv_bias: bfloat16 [2, 1536], replicated, may hold values from -4 to 4
- out_weight: bfloat16 [2, 768, 768], P(None, 'dp'), may hold values from -1.25 to 1.25
- rel_table: bfloat16 [2, 12, 732], replicated, may hold values from -6 to 6
- up_weight: bfloat16 [2, 768, 3072], P(None, 'dp'), may hold values from -0.21875 to 0.21875
- up_bias: bfloat16 [2, 3072], replicated, may hold values from -4 to 4
- down_weight: bfloat16 [2, 3072, 768], P(None, 'dp'), may hold values from -0.109375 to 0.109375
- cotangent: bfloat16 [16, 197, 768], P('dp'), may hold values from -6 to 6
Outputs:
- block_out: bfloat16 [16, 197, 768], P('dp', None, 'section')
- input_grad: float32 [16, 197, 768], P('dp', None, 'section')
- qkv_grad: float32 [2, 768, 2304], P(None, 'dp', 'section')
- out_grad: float32 [2, 768, 768], P(None, 'dp', 'section')
- up_grad: float32 [2, 768, 3072], P(None, 'dp', 'section')
- down_grad: float32 [2, 3072, 768], P(None, 'dp', 'section')
- qv_bias_grad: float32 [2, 1536], replicated
- up_bias_grad: float32 [2, 3072], replicated
- table_grad: float32 [2, 12, 732], replicated
- gain_grad: float32 [4, 768], P('section')
- shift_grad: float32 [4, 768], P('section')
- scale_grad: float32 [4, 768], P('section')
- bias_grad: float32 [4, 768], P('section')
- mask_token_grad: float32 [768], replicated
Inputs may be any that keep to these rules, and one draw needn't show every extreme that they name: `page_mask`: each page masks its patches independently, with a probability of its own drawn per page between 20 and 60 percent.
All inputs are finite; a program needn't handle non-finite values.
Results may differ from a plain program's by a relative error of at most 0.018.
Values may be sent and summed in bfloat16 or wider, within the bound.
A program may use at most 256 MiB of HBM per device.

v0:
```python
import jax
import jax.numpy as jnp
from jax import lax
from jax.sharding import PartitionSpec as P

LAYERS = 2
MICRO = 2


eps_norm = 1e-06


def for_sending(x):
    return jax.tree.map(lambda a: a.astype(jnp.bfloat16) if a.dtype == jnp.float32 else a, x)


def passed_along(value, axis, steps):
    count = lax.axis_size(axis)
    initial, last = (max(0, -steps), min(count, count - steps))
    return lax.ppermute(value, axis, [(source, source + steps) for source in range(initial, last)])


def norm_rows(values, gain_row, shift_row):
    row_mean = jnp.mean(values, -1, keepdims=True)
    centered = values - row_mean
    spread = jnp.mean(centered * centered, -1, keepdims=True)
    return centered * lax.rsqrt(spread + eps_norm) * gain_row + shift_row


def smooth_gate(pre_value):
    return jax.nn.gelu(pre_value, approximate=True)


def pick_layer(stacked, layer_index):
    return lax.dynamic_index_in_dim(stacked, layer_index, 0, keepdims=False)


def times_plain(left_side, right_side):
    return jnp.dot(left_side, right_side, preferred_element_type=jnp.float32)


def times_transposed(left_side, right_side):
    return lax.dot_general(
        left_side, right_side, (((1,), (1,)), ((), ())), preferred_element_type=jnp.float32
    )


def transposed_times(left_side, right_side):
    return lax.dot_general(
        left_side, right_side, (((0,), (0,)), ((), ())), preferred_element_type=jnp.float32
    )


def per_device(
    patches,
    page_mask,
    mask_token,
    buckets,
    ln_gain,
    ln_shift,
    layer_scale,
    branch_bias,
    qkv_weight,
    qv_bias,
    out_weight,
    rel_table,
    up_weight,
    up_bias,
    down_weight,
    cotangent,
):
    sections = lax.axis_size("section")
    section_index = lax.axis_index("section")
    layer_index = section_index // 2
    attention_section = section_index % 2 == 0
    pages_dev, page_rows, model_width = patches.shape
    head_count = rel_table.shape[1]
    head_size = model_width // head_count
    hidden = up_weight.shape[2]
    bucket_count = rel_table.shape[2]
    pages_micro = pages_dev // MICRO
    micro_rows = pages_micro * page_rows
    score_scale = head_size ** (-0.5)
    split_shape = (pages_micro, page_rows, head_count, head_size)
    own_qkv = pick_layer(qkv_weight, layer_index)
    own_out = pick_layer(out_weight, layer_index)
    own_up = pick_layer(up_weight, layer_index)
    own_down = pick_layer(down_weight, layer_index)
    first_part = jnp.where(attention_section, jnp.concatenate([own_qkv, own_out], 1), own_up)
    second_part = jnp.where(
        attention_section, jnp.zeros_like(own_up), own_down.reshape(own_up.shape)
    )
    first_whole, second_whole = (
        lax.all_gather(first_part, "dp", axis=0, tiled=True),
        lax.all_gather(second_part, "dp", axis=0, tiled=True),
    )
    w_qkv = first_whole[:, : 3 * model_width]
    w_out = first_whole[:, 3 * model_width :]
    w_down = second_whole.reshape(hidden, model_width)
    gain_row = ln_gain[0].astype(jnp.float32)
    shift_row = ln_shift[0].astype(jnp.float32)
    scale_row = layer_scale[0].astype(jnp.float32)
    bias_row = branch_bias[0].astype(jnp.float32)
    query_value_bias = pick_layer(qv_bias, layer_index).astype(jnp.float32)
    hidden_bias = pick_layer(up_bias, layer_index).astype(jnp.float32)
    table_now = pick_layer(rel_table, layer_index).astype(jnp.float32)
    position_bias = jnp.take(table_now, buckets, axis=1)

    def attention_parts(inputs):
        normed = norm_rows(inputs, gain_row, shift_row).astype(jnp.bfloat16)
        projected = times_plain(normed, w_qkv)
        query_heads = (
            (projected[:, :model_width] + query_value_bias[:model_width])
            .astype(jnp.bfloat16)
            .reshape(split_shape)
        )
        key_heads = (
            projected[:, model_width : 2 * model_width].astype(jnp.bfloat16).reshape(split_shape)
        )
        value_heads = (
            (projected[:, 2 * model_width :] + query_value_bias[model_width:])
            .astype(jnp.bfloat16)
            .reshape(split_shape)
        )
        raw_scores = jnp.einsum(
            "pihd,pjhd->phij", query_heads, key_heads, preferred_element_type=jnp.float32
        )
        attention_probs = jax.nn.softmax(raw_scores * score_scale + position_bias[None], axis=-1)
        probs_low = attention_probs.astype(jnp.bfloat16)
        context = jnp.einsum(
            "phij,pjhd->pihd", probs_low, value_heads, preferred_element_type=jnp.float32
        )
        context = context.reshape(micro_rows, model_width).astype(jnp.bfloat16)
        branch = times_plain(context, w_out) + bias_row
        return (
            normed,
            query_heads,
            key_heads,
            value_heads,
            attention_probs,
            probs_low,
            context,
            branch,
        )

    def mlp_parts(inputs):
        normed = norm_rows(inputs, gain_row, shift_row).astype(jnp.bfloat16)
        pre_act = times_plain(normed, first_whole) + hidden_bias
        activated = smooth_gate(pre_act).astype(jnp.bfloat16)
        branch = times_plain(activated, w_down) + bias_row
        return (normed, pre_act, activated, branch)

    def attention_forward(entering):
        inputs = entering.astype(jnp.float32)
        branch = attention_parts(inputs)[7]
        return (inputs + scale_row * branch).astype(jnp.bfloat16)

    def mlp_forward(entering):
        inputs = entering.astype(jnp.float32)
        branch = mlp_parts(inputs)[3]
        return (inputs + scale_row * branch).astype(jnp.bfloat16)

    def forward_skip(entering):
        return jnp.zeros_like(entering)

    def add_attention(matrices, qkv_part, out_part):
        return (matrices[0] + jnp.concatenate([qkv_part, out_part], 1), matrices[1])

    def add_mlp(matrices, up_part, down_part):
        return (matrices[0] + up_part, matrices[1] + down_part.reshape(model_width, hidden))

    def finish_norm(inputs, normed_grad, grad_out):
        unused_value, norm_back = jax.vjp(norm_rows, inputs, gain_row, shift_row)
        input_part, gain_part, shift_part = norm_back(normed_grad)
        return (input_part + grad_out, gain_part, shift_part)

    def attention_backward(stored, grad_low, accumulated):
        matrices, smalls = accumulated
        inputs = stored.astype(jnp.float32)
        normed, query_heads, key_heads, value_heads, attention_probs, probs_low, context, branch = (
            attention_parts(inputs)
        )
        grad_out = grad_low.astype(jnp.float32)
        scale_part = jnp.sum(grad_out * branch, 0)
        branch_grad = (grad_out * scale_row).astype(jnp.bfloat16)
        bias_part = jnp.sum(branch_grad.astype(jnp.float32), 0)
        out_part = transposed_times(context, branch_grad)
        context_grad = (
            times_transposed(branch_grad, w_out).astype(jnp.bfloat16).reshape(split_shape)
        )
        prob_grad = jnp.einsum(
            "pihd,pjhd->phij", context_grad, value_heads, preferred_element_type=jnp.float32
        )
        score_grad = (
            attention_probs * (prob_grad - jnp.sum(attention_probs * prob_grad, -1, keepdims=True))
        ).astype(jnp.bfloat16)
        table_part = jnp.sum(score_grad.astype(jnp.float32), 0)
        query_grad = (
            jnp.einsum("phij,pjhd->pihd", score_grad, key_heads, preferred_element_type=jnp.float32)
            * score_scale
        ).astype(jnp.bfloat16)
        key_grad = (
            jnp.einsum(
                "phij,pihd->pjhd", score_grad, query_heads, preferred_element_type=jnp.float32
            )
            * score_scale
        ).astype(jnp.bfloat16)
        value_grad = jnp.einsum(
            "phij,pihd->pjhd", probs_low, context_grad, preferred_element_type=jnp.float32
        ).astype(jnp.bfloat16)
        projected_grad = jnp.concatenate(
            [
                query_grad.reshape(micro_rows, model_width),
                key_grad.reshape(micro_rows, model_width),
                value_grad.reshape(micro_rows, model_width),
            ],
            1,
        )
        qv_part = jnp.concatenate(
            [
                jnp.sum(query_grad.astype(jnp.float32), (0, 1)).reshape(-1),
                jnp.sum(value_grad.astype(jnp.float32), (0, 1)).reshape(-1),
            ]
        )
        qkv_part = transposed_times(normed, projected_grad)
        normed_grad = times_transposed(projected_grad, w_qkv)
        input_grad, gain_part, shift_part = finish_norm(inputs, normed_grad, grad_out)
        new_smalls = (
            smalls[0] + gain_part,
            smalls[1] + shift_part,
            smalls[2] + scale_part,
            smalls[3] + bias_part,
            smalls[4] + qv_part,
            smalls[5],
            smalls[6] + table_part,
        )
        return (input_grad, (add_attention(matrices, qkv_part, out_part), new_smalls))

    def mlp_backward(stored, grad_low, accumulated):
        matrices, smalls = accumulated
        inputs = stored.astype(jnp.float32)
        normed, pre_act, activated, branch = mlp_parts(inputs)
        grad_out = grad_low.astype(jnp.float32)
        scale_part = jnp.sum(grad_out * branch, 0)
        branch_grad = (grad_out * scale_row).astype(jnp.bfloat16)
        bias_part = jnp.sum(branch_grad.astype(jnp.float32), 0)
        down_part = transposed_times(activated, branch_grad)
        act_grad = times_transposed(branch_grad, w_down)
        unused_value, gate_back = jax.vjp(smooth_gate, pre_act)
        pre_grad = gate_back(act_grad)[0].astype(jnp.bfloat16)
        up_bias_part = jnp.sum(pre_grad.astype(jnp.float32), 0)
        up_part = transposed_times(normed, pre_grad)
        normed_grad = times_transposed(pre_grad, first_whole)
        input_grad, gain_part, shift_part = finish_norm(inputs, normed_grad, grad_out)
        new_smalls = (
            smalls[0] + gain_part,
            smalls[1] + shift_part,
            smalls[2] + scale_part,
            smalls[3] + bias_part,
            smalls[4],
            smalls[5] + up_bias_part,
            smalls[6],
        )
        return (input_grad, (add_mlp(matrices, up_part, down_part), new_smalls))

    def backward_skip(stored, grad_low, accumulated):
        return (jnp.zeros((micro_rows, model_width), jnp.float32), accumulated)

    start_rows = jnp.where(page_mask[..., None] == 1, mask_token, patches)
    saved_inputs = jnp.zeros((MICRO, micro_rows, model_width), jnp.bfloat16)
    finished = jnp.zeros((MICRO, micro_rows, model_width), jnp.bfloat16)
    arriving = jnp.zeros((micro_rows, model_width), jnp.bfloat16)
    time_steps = MICRO + sections - 1
    for time_step in range(time_steps):
        micro_slot = time_step - section_index
        is_live = (micro_slot >= 0) & (micro_slot < MICRO)
        slot_safe = jnp.clip(micro_slot, 0, MICRO - 1)
        entering = jnp.where(
            section_index == 0,
            lax.dynamic_index_in_dim(start_rows, slot_safe, 0, keepdims=False),
            arriving,
        )
        saved_inputs = jnp.where(
            is_live,
            lax.dynamic_update_index_in_dim(saved_inputs, entering, slot_safe, 0),
            saved_inputs,
        )
        branch_index = jnp.where(is_live, 1 + section_index % 2, 0)
        leaving = lax.switch(branch_index, [forward_skip, attention_forward, mlp_forward], entering)
        finished = jnp.where(
            is_live & (section_index == sections - 1),
            lax.dynamic_update_index_in_dim(finished, leaving, slot_safe, 0),
            finished,
        )
        if time_step + 1 < time_steps:
            arriving = jax.tree.map(
                lambda part, own: part.astype(own.dtype),
                passed_along(for_sending(leaving), "section", 1),
                leaving,
            )
    matrices = (
        jnp.zeros((model_width, hidden), jnp.float32),
        jnp.zeros((model_width, hidden), jnp.float32),
    )
    feature_zeros = jnp.zeros((model_width,), jnp.float32)
    smalls = (
        feature_zeros,
        feature_zeros,
        feature_zeros,
        feature_zeros,
        jnp.zeros((2 * model_width,), jnp.float32),
        jnp.zeros((hidden,), jnp.float32),
        jnp.zeros((head_count, page_rows, page_rows), jnp.float32),
    )
    accumulated = (matrices, smalls)
    input_grads = jnp.zeros((MICRO, micro_rows, model_width), jnp.float32)
    returning = jnp.zeros((micro_rows, model_width), jnp.bfloat16)
    for time_step in range(time_steps):
        micro_slot = time_step - (sections - 1 - section_index)
        is_live = (micro_slot >= 0) & (micro_slot < MICRO)
        slot_safe = jnp.clip(micro_slot, 0, MICRO - 1)
        grad_in = jnp.where(
            section_index == sections - 1,
            lax.dynamic_index_in_dim(cotangent, slot_safe, 0, keepdims=False),
            returning,
        )
        stored = lax.dynamic_index_in_dim(saved_inputs, slot_safe, 0, keepdims=False)
        branch_index = jnp.where(is_live, 1 + section_index % 2, 0)
        input_grad, accumulated = lax.switch(
            branch_index,
            [backward_skip, attention_backward, mlp_backward],
            stored,
            grad_in,
            accumulated,
        )
        input_grads = jnp.where(
            is_live & (section_index == 0),
            lax.dynamic_update_index_in_dim(input_grads, input_grad, slot_safe, 0),
            input_grads,
        )
        if time_step + 1 < time_steps:
            returning = passed_along(input_grad.astype(jnp.bfloat16), "section", -1)
    matrices, smalls = accumulated
    first_sum, second_sum = (
        lax.psum_scatter(matrices[0], "dp", scatter_dimension=0, tiled=True),
        lax.psum_scatter(matrices[1], "dp", scatter_dimension=0, tiled=True),
    )
    qkv_sum = jnp.where(attention_section, first_sum[:, : 3 * model_width], 0.0)
    out_sum = jnp.where(attention_section, first_sum[:, 3 * model_width :], 0.0)
    up_sum = jnp.where(attention_section, 0.0, first_sum)
    down_sum = jnp.where(attention_section, 0.0, second_sum.reshape(-1, model_width))
    layer_pick = (jnp.arange(LAYERS) == layer_index).astype(jnp.float32)
    half_pick = (jnp.arange(sections) == section_index).astype(jnp.float32)
    block_full = finished.astype(jnp.float32)
    masked = page_mask[..., None] == 1
    kept_grad = jnp.where(masked, 0.0, input_grads)
    token_grad = jnp.sum(jnp.where(masked, input_grads, 0.0), (0, 1))
    qkv_out, out_out, up_out, down_out, block_out, input_out = (
        lax.psum_scatter(
            layer_pick[:, None, None] * qkv_sum[None], "section", scatter_dimension=2, tiled=True
        ),
        lax.psum_scatter(
            layer_pick[:, None, None] * out_sum[None], "section", scatter_dimension=2, tiled=True
        ),
        lax.psum_scatter(
            layer_pick[:, None, None] * up_sum[None], "section", scatter_dimension=2, tiled=True
        ),
        lax.psum_scatter(
            layer_pick[:, None, None] * down_sum[None], "section", scatter_dimension=2, tiled=True
        ),
        lax.psum_scatter(block_full, "section", scatter_dimension=2, tiled=True),
        lax.psum_scatter(kept_grad, "section", scatter_dimension=2, tiled=True),
    )
    table_pairs = smalls[6].reshape(head_count, page_rows * page_rows).T
    table_local = jax.ops.segment_sum(table_pairs, buckets.reshape(-1), num_segments=bucket_count).T
    (
        gain_total,
        shift_total,
        scale_total,
        bias_total,
        qv_total,
        up_bias_total,
        table_total,
        token_total,
    ) = lax.psum(
        (
            half_pick[:, None] * smalls[0][None],
            half_pick[:, None] * smalls[1][None],
            half_pick[:, None] * smalls[2][None],
            half_pick[:, None] * smalls[3][None],
            layer_pick[:, None] * smalls[4][None],
            layer_pick[:, None] * smalls[5][None],
            layer_pick[:, None, None] * table_local[None],
            token_grad,
        ),
        ("section", "dp"),
    )

    def own_row(total_rows):
        return lax.dynamic_slice_in_dim(total_rows, section_index, 1, 0)

    return (
        block_out.astype(jnp.bfloat16),
        input_out,
        qkv_out,
        out_out,
        up_out,
        down_out,
        qv_total,
        up_bias_total,
        table_total,
        own_row(gain_total),
        own_row(shift_total),
        own_row(scale_total),
        own_row(bias_total),
        token_total,
    )


def solution(mesh):
    in_specs = (
        P("dp", None, None),
        P("dp", None),
        P(),
        P(),
        P("section", None),
        P("section", None),
        P("section", None),
        P("section", None),
        P(None, "dp", None),
        P(),
        P(None, "dp", None),
        P(),
        P(None, "dp", None),
        P(),
        P(None, "dp", None),
        P("dp", None, None),
    )
    out_specs = (
        P("dp", None, "section"),
        P("dp", None, "section"),
        P(None, "dp", "section"),
        P(None, "dp", "section"),
        P(None, "dp", "section"),
        P(None, "dp", "section"),
        P(),
        P(),
        P(),
        P("section", None),
        P("section", None),
        P("section", None),
        P("section", None),
        P(),
    )
    return jax.shard_map(
        per_device, mesh=mesh, in_specs=in_specs, out_specs=out_specs, check_vma=False
    )
```

profile of v0, /device:TPU:0, one launch (start us, length us, event | category | flops | bytes accessed | tf_op | source)
XLA Modules:
  0.0 1501.9 jit_solution(6306897410400916753)
XLA Ops:
  12.6 128.5 %gather_fusion = f32[38809,12]{1,0:T(8,128)} fusion(f32[12,732]{0,1:T(8,128)S(1)} %bitcast_convert_fusion, s32[38912]{0:T(1024)S(1)} %pad_clamp_fusion), kind=kCustom, calls=%fused_computation | custom fusion | bytes 3880900 | tf_op jit(solution)/shard_map/jit(_take)/gather | solution.py:107
  141.1 11.1 copy.304
  165.0 9.2 all-gather.5.cloned.1.call-done
  174.2 8.5 reshape.1312
  182.7 39.0 %conditional.10 = (bf16[197,768]{1,0:T(8,128)(2,1)}, bf16[1,197,768]{2,1,0:T(8,128)(2,1)}) conditional(s32[]{:T(128)} %clamp.30, () %tuple.143, (bf16[197,768]{1,0:T(8,128)(2,1)}, f32[768]{0:T(1024)S(1)}, f32[768]{0:T(1024)S(1)}, f32[768]{0:T(1024)S(1)}, bf16[768,2304]{1,0:T(8,128)(2,1)S(1)}, /*index=5*/f32[1536]{0:T(1024)}, ...), branch_computations={%region_0.1_spmd, %region_1.6_spmd, %region_6.9_spmd} | conditional | flops 1867749376 | bytes 40373464 | solution.py:289
  191.0 3.3 copy.305
  204.9 4.0 convolution_convert_fusion
  226.5 27.7 %conditional.11 = (bf16[197,768]{1,0:T(8,128)(2,1)}, bf16[1,197,768]{2,1,0:T(8,128)(2,1)}) conditional(s32[]{:T(128)} %clamp.31, () %tuple.146, (bf16[197,768]{1,0:T(8,128)(2,1)S(1)}, f32[768]{0:T(1024)S(1)}, f32[768]{0:T(1024)S(1)}, f32[768]{0:T(1024)S(1)}, bf16[768,2304]{1,0:T(8,128)(2,1)S(1)}, /*index=5*/f32[1536]{0:T(1024)}, ...), branch_computations={%region_9.10_spmd, %region_10.15_spmd, %region_15.18_spmd} | conditional | flops 1867749376 | bytes 41596176 | solution.py:289
  231.9 3.3 copy.306
  245.8 4.0 convolution_convert_fusion.1
  258.9 10.6 conditional.12
  269.5 3.7 collective-permute-start.2
  277.3 19.7 %collective-permute-start.3 = (bf16[197,768]{1,0:T(8,128)(2,1)}, bf16[197,768]{1,0:T(8,128)(2,1)}, u32[]{:S(2)}, u32[]{:S(2)}) collective-permute-start(bf16[197,768]{1,0:T(8,128)(2,1)} %get-tuple-element.957), channel_id=1, source_target_pairs={{0,8},{8,16},{16,24},{1,9},{9,17},{17,25},{2,10},{10,18},{18,26},{... | collective-permute-start | bytes 907784 | tf_op jit(solution)/shard_map/ppermute | solution.py:20
  297.0 6.7 constant_dynamic-slice_fusion.8
  309.7 23.5 %conditional.15 = (f32[197,768]{1,0:T(8,128)}, f32[768,3072]{1,0:T(8,128)}, f32[768,3072]{1,0:T(8,128)}, f32[768]{0:T(1024)S(1)}, f32[768]{0:T(1024)}, /*index=5...) conditional(s32[]{:T(128)} %clamp.35, () %tuple.158, ...), branch_computations={%region_46.47_spmd, %region_47.61_spmd, %region_61.71_spmd} | conditional | flops 5611110400 | bytes 141796784 | solution.py:329
  310.6 4.8 broadcast.1129
  315.4 4.8 broadcast.1129.clone
  336.3 29.9 %collective-permute-done.4 = bf16[197,768]{1,0:T(8,128)(2,1)} collective-permute-done((bf16[197,768]{1,0:T(8,128)(2,1)}, bf16[197,768]{1,0:T(8,128)(2,1)}, u32[]{:S(2)}, u32[]{:S(2)}) %collective-permute-start.4) | collective-permute-done | bytes 302624 | tf_op jit(solution)/shard_map/ppermute | solution.py:20
  368.1 9.1 conditional.16
  380.3 7.2 collective-permute-done.5
  389.4 9.2 conditional.17
  401.8 153.3 %collective-permute-done.6 = bf16[197,768]{1,0:T(8,128)(2,1)} collective-permute-done((bf16[197,768]{1,0:T(8,128)(2,1)}, bf16[197,768]{1,0:T(8,128)(2,1)}, u32[]{:S(2)}, u32[]{:S(2)}) %collective-permute-start.6) | collective-permute-done | bytes 302624 | tf_op jit(solution)/shard_map/ppermute | solution.py:20
  557.0 80.3 %conditional.18 = (f32[197,768]{1,0:T(8,128)}, f32[768,3072]{1,0:T(8,128)}, f32[768,3072]{1,0:T(8,128)}, f32[768]{0:T(1024)S(1)}, f32[768]{0:T(1024)}, /*index=5...) conditional(s32[]{:T(128)} %clamp.38, (f32[768,3072]{1,0:T(8,128)}, ...), branch_computations={%region_121.122_spmd, %region_122.136_spmd, %region_136.146_spmd} | conditional | flops 5615835136 | bytes 157585168 | solution.py:329
  583.3 4.6 convert_reduce_fusion.31
  592.5 4.0 convert_add_fusion.8
  603.7 4.0 convolution_convert_fusion.14
  610.9 8.8 maximum_add_fusion.4
  640.5 5.3 collective-permute-done.7
  647.8 75.0 %conditional.19 = (f32[768,3072]{1,0:T(8,128)}, f32[768,3072]{1,0:T(8,128)}, f32[768]{0:T(1024)S(1)}, f32[768]{0:T(1024)}, f32[768]{0:T(1024)}, /*index=5*/f32[7...) conditional(s32[]{:T(128)} %clamp.39, (f32[768,3072]{1,0:T(8,128)}, ...), branch_computations={%region_146.147_spmd, %region_147.161_spmd, %region_161.171_spmd} | conditional | flops 5615835136 | bytes 156885520 | solution.py:329
  670.9 4.0 convolution_convert_fusion.17
  681.1 4.7 convert_reduce_fusion.38
  688.5 3.8 convert_add_fusion.11
  695.6 8.8 maximum_add_fusion.6
  734.5 3.5 copy.321
  738.1 145.4 %reduce-scatter.11.cloned.1.call-done = f32[96,3072]{1,0:T(8,128)} async-done(((f32[768,3072]{1,0:T(8,128)}), f32[96,3072]{1,0:T(8,128)}) %reduce-scatter.11.cloned.1.call-update) | async-done | bytes 1179664 | tf_op jit(solution)/shard_map/reduce_scatter | solution.py:345
  892.7 4.2 copy.358
  896.9 3.9 reshape.1340
  906.1 3.8 reshape.1313
  909.9 11.0 copy.324
  920.9 208.0 %scatter_custom_fusion = f32[732,12]{1,0:T(8,128)} fusion(s32[38809]{0:T(1024)} %reshape.1331, f32[38809,12]{1,0:T(8,128)} %copy.324, f32[]{:T(128)} %constant.566.clone.1), kind=kCustom, calls=%fused_computation.882 | custom fusion | flops 465708 | bytes 35648 | tf_op jit(solution)/shard_map/scatter-add | solution.py:375
  1146.8 3.3 conditional.14
  1154.1 47.4 %all-reduce.13 = bf16[2,197,768]{1,0,2:T(2,128)(2,1)S(1)} all-reduce(f32[2,197,768]{1,0,2:T(2,128)S(1)} %copy.310), channel_id=2, replica_groups=mesh['section'=4,'dp'=8] {'section'}, use_global_device_ids=true, to_apply=%region_45.46.clone | all-reduce | flops 302592 | bytes 1815552
  1207.5 22.6 %all-reduce.10.cloned.1.call-done = f32[2,197,768]{1,0,2:T(2,128)} async-done(((f32[2,197,768]{1,0,2:T(2,128)}), f32[2,197,768]{1,0,2:T(2,128)}) %all-reduce.10.cloned.1.call-update) | async-done | bytes 1210384
  1232.1 24.1 %reduce-scatter.21.cloned.1.call-done = f32[192,192]{1,0:T(8,128)} async-done(((f32[768,192]{1,0:T(8,128)}), f32[192,192]{1,0:T(8,128)}) %reduce-scatter.21.cloned.1.call-update) | async-done | bytes 147472
  1258.1 33.7 %reduce-scatter.19.cloned.1.call-done = f32[576,192]{1,0:T(8,128)} async-done(((f32[2304,192]{1,0:T(8,128)}), f32[576,192]{1,0:T(8,128)}) %reduce-scatter.19.cloned.1.call-update) | async-done | bytes 442384
  1294.3 123.0 %all-reduce.8.cloned.1.call-done = f32[2,12,732]{2,0,1:T(2,128)} async-done(((f32[2,12,732]{2,0,1:T(2,128)}), f32[2,12,732]{2,0,1:T(2,128)}) %all-reduce.8.cloned.1.call-update) | async-done | bytes 70288 | tf_op jit(solution)/shard_map/psum | solution.py:385
  1417.3 38.1 %reduce-scatter.13.cloned.1.call-done = f32[2,96,768]{2,1,0:T(8,128)} async-done(((f32[2,96,3072]{2,1,0:T(8,128)}), f32[2,96,768]{2,1,0:T(8,128)}) %reduce-scatter.13.cloned.1.call-update) | async-done | bytes 589840 | tf_op jit(solution)/shard_map/reduce_scatter | solution.py:365
  1455.4 36.2 %reduce-scatter.17.cloned.1.call-done = f32[2,384,192]{1,2,0:T(8,128)} async-done(((f32[2,384,768]{1,2,0:T(8,128)}), f32[2,384,192]{1,2,0:T(8,128)}) %reduce-scatter.17.cloned.1.call-update) | async-done | bytes 589840 | tf_op jit(solution)/shard_map/reduce_scatter | solution.py:368
  (409 shorter events, 271.6 us)
Async XLA Ops:
  7.2 153.2 %all-gather.3.cloned.1.call-start = ((), (), s32[]{:S(2)}) async-start(), calls=%async_computation.6 | async-start | bytes 5308416 | tf_op jit(solution)/shard_map/all_gather | solution.py:94
  8.5 3.5 copy-start.155
  8.5 3.7 copy-start.95
  10.6 163.6 %all-gather.5.cloned.1.call-start = ((), (), s32[]{:S(2)}) async-start(), calls=%async_computation.7 | async-start | bytes 5308416 | tf_op jit(solution)/shard_map/all_gather | solution.py:95
  11.9 871.6 %reduce-scatter.11.cloned.1.call-start = ((), (), s32[]{:S(2)}) async-start(), calls=%async_computation.8 | async-start | bytes 10616832 | tf_op jit(solution)/shard_map/reduce_scatter | solution.py:345
  152.2 3.5 copy-start.221
  152.2 3.5 copy-start.223
  152.2 3.5 copy-start.224
  152.3 3.5 copy-start.226
  152.3 3.6 copy-start.225
  155.1 3.7 copy-start.51
  155.8 26.9 %copy-start.205 = (f32[768]{0:T(1024)}, f32[768]{0:T(1024)S(1)}, u32[]{:S(2)}) copy-start(f32[768]{0:T(1024)S(1)} %get-tuple-element.1605) | copy-start | bytes 9220
  221.7 2.9 collective-permute-start
  245.8 4.0 copy-start.208
  254.1 2.8 collective-permute-start.1
  269.5 4.5 collective-permute-start.2
  277.3 27.5 %collective-permute-start.3 = (bf16[197,768]{1,0:T(8,128)(2,1)}, bf16[197,768]{1,0:T(8,128)(2,1)}, u32[]{:S(2)}, u32[]{:S(2)}) collective-permute-start(bf16[197,768]{1,0:T(8,128)(2,1)} %get-tuple-element.957), channel_id=1, source_target_pairs={{0,8},{8,16},{16,24},{1,9},{9,17},{17,25},{2,10},{10,18},{18,26},{... | collective-permute-start | bytes 907784 | tf_op jit(solution)/shard_map/ppermute | solution.py:20
  304.8 4.9 copy-start.20
  335.0 31.2 %collective-permute-start.4 = (bf16[197,768]{1,0:T(8,128)(2,1)}, bf16[197,768]{1,0:T(8,128)(2,1)}, u32[]{:S(2)}, u32[]{:S(2)}) collective-permute-start(bf16[197,768]{1,0:T(8,128)(2,1)} %convert_element_type.844), channel_id=1, source_target_pairs={{8,0},{16,8},{24,16},{9,1},{17,9},{25,17},{10,2},{18,10},{26,18},{... | collective-permute-start | bytes 907784 | tf_op jit(solution)/shard_map/ppermute | solution.py:20
  379.0 8.5 collective-permute-start.5
  400.5 154.6 %collective-permute-start.6 = (bf16[197,768]{1,0:T(8,128)(2,1)}, bf16[197,768]{1,0:T(8,128)(2,1)}, u32[]{:S(2)}, u32[]{:S(2)}) collective-permute-start(bf16[197,768]{1,0:T(8,128)(2,1)} %convert_element_type.846), channel_id=1, source_target_pairs={{8,0},{16,8},{24,16},{9,1},{17,9},{25,17},{10,2},{18,10},{26,18},{... | collective-permute-start | bytes 907784 | tf_op jit(solution)/shard_map/ppermute | solution.py:20
  592.5 4.0 copy-start.91
  592.5 4.6 copy-start.92
  610.8 8.9 copy-start.183
  610.8 8.9 copy-start.219
  610.8 10.2 copy-start.25
  610.8 10.2 copy-start.135
  610.9 10.2 copy-start.214
  610.9 12.9 copy-start.177
  639.2 6.6 collective-permute-start.7
  648.9 3.8 copy-start.143
  688.5 3.9 copy-start.85
  688.5 4.4 copy-start.86
  722.8 411.5 %reduce-scatter.15.cloned.1.call-start = ((), (), s32[]{:S(2)}) async-start(), calls=%async_computation.10 | async-start | bytes 10616832 | tf_op jit(solution)/shard_map/reduce_scatter | solution.py:346
  723.3 479.0 %all-reduce.12.cloned.1.call-start = ((), (), s32[]{:S(2)}) async-start(), calls=%async_computation.16 | async-start | bytes 180224 | tf_op jit(solution)/shard_map/psum | solution.py:385
  723.4 9.6 copy-start.172
  724.8 5.0 copy-start.191
  734.4 495.7 %all-reduce.10.cloned.1.call-start = ((), (), s32[]{:S(2)}) async-start(), calls=%async_computation.15 | async-start | bytes 3145728
  734.5 150.0 %copy-start.173 = (f32[2]{0:T(128)S(1)}, f32[2]{0:T(128)}, u32[]{:S(2)}) copy-start(f32[2]{0:T(128)} %copy-done.172) | copy-start | bytes 28
  738.0 518.2 %reduce-scatter.21.cloned.1.call-start = ((), (), s32[]{:S(2)}) async-start(), calls=%async_computation.14 | async-start | bytes 983040
  890.0 401.9 %reduce-scatter.19.cloned.1.call-start = ((), (), s32[]{:S(2)}) async-start(), calls=%async_computation.13 | async-start | bytes 2949120
  900.9 516.4 %all-reduce.8.cloned.1.call-start = ((), (), s32[]{:S(2)}) async-start(), calls=%async_computation.12 | async-start | bytes 147456 | tf_op jit(solution)/shard_map/psum | solution.py:385
  1132.2 323.1 %reduce-scatter.13.cloned.1.call-start = ((), (), s32[]{:S(2)}) async-start(), calls=%async_computation.9 | async-start | bytes 2949120 | tf_op jit(solution)/shard_map/reduce_scatter | solution.py:365
  1134.2 357.4 %reduce-scatter.17.cloned.1.call-start = ((), (), s32[]{:S(2)}) async-start(), calls=%async_computation.11 | async-start | bytes 2949120 | tf_op jit(solution)/shard_map/reduce_scatter | solution.py:368
  1201.6 293.2 %copy-start.1 = (bf16[2,96,2304]{2,1,0:T(8,128)(2,1)S(1)}, bf16[2,96,2304]{2,1,0:T(8,128)(2,1)}, u32[]{:S(2)}) copy-start(bf16[2,96,2304]{2,1,0:T(8,128)(2,1)} %param.54) | copy-start | bytes 2654212
  1202.3 289.2 %copy-start.185 = (f32[2,1536]{1,0:T(2,128)S(1)}, f32[2,1536]{1,0:T(2,128)}, u32[]{:S(2)}) copy-start(f32[2,1536]{1,0:T(2,128)} %get-tuple-element.1789) | copy-start | bytes 36868
  1202.3 289.8 %copy-start.174 = (f32[2,3072]{1,0:T(2,128)S(1)}, f32[2,3072]{1,0:T(2,128)}, u32[]{:S(2)}) copy-start(f32[2,3072]{1,0:T(2,128)} %get-tuple-element.1790) | copy-start | bytes 73732
  1202.3 291.9 %copy-start.220 = (f32[768]{0:T(1024)S(1)}, f32[768]{0:T(1024)}, u32[]{:S(2)}) copy-start(f32[768]{0:T(1024)} %get-tuple-element.1796) | copy-start | bytes 9220
  (56 other events, 111.9 us)
Sparse Core Ops, SparseCore 0:
  10.8 82.5 all-gather.2
  96.2 78.0 all-gather.4
  722.9 160.5 reduce-scatter.10
  886.9 162.5 reduce-scatter.14
  1056.3 122.8 all-reduce.11
  1181.6 48.4 all-reduce.9
  1232.9 23.3 reduce-scatter.20
  1258.8 33.0 reduce-scatter.18
  1298.9 118.3 all-reduce.7
  1420.4 34.9 reduce-scatter.12
  1458.5 33.0 reduce-scatter.16
where the time goes:
time: 1510 us; the launch traced here: 1500 us
  waiting for transfers between devices  631 us (42%)
  other arithmetic  324 us (21%)
  local copies, waits for them, and re-layouts  317 us (21%)
  matrix products  72.3 us (5%)
  loops' own time  60.9 us (4%)
  blocking collectives  47.4 us (3%)
  starting transfers between devices  33 us (2%)
  between operations  15.8 us (1%)
    scatter-add x1, other arithmetic, per_device(): jax.ops.segment_sum(table_pairs, buckets.reshape(-1), num_segments=bucket...  208 us
    ppermute x8, waiting for transfers between devices, passed_along(): lax.ppermute(value, axis, [(source, source + steps) for source in range(i...  198 us
    reduce_scatter x1, waiting for transfers between devices, per_device(): lax.psum_scatter(matrices[0], 'dp', scatter_dimension=0, tiled=True)  145 us
    gather x3, local copies, waits for them, and re-layouts, per_device(): position_bias = jnp.take(table_now, buckets, axis=1)  142 us
    psum x2, waiting for transfers between devices, per_device(): lax.psum((half_pick[:, None] * smalls[0][None], half_pick[:, None] * smal...  123 us
    unnamed x14, waiting for transfers between devices  81.2 us
    unnamed x1, blocking collectives  47.4 us
    another operation x5, loops' own time, per_device(): lax.switch(branch_index, [backward_skip, attention_backward, mlp_backward...  40.7 us
  transfers between devices with their start and end apart: 19, of which 15 were waited for; matrix products, arithmetic and copies ran while one was open for 30% of the time, Pallas kernels for 0%

commit v1 on v0

v1 whole, which is shorter than its diff:
```python
import functools

import jax
import jax.numpy as jnp
from jax import lax
from jax.experimental import pallas as pl
from jax.experimental.pallas import tpu as pltpu
from jax.sharding import PartitionSpec as P

EPS = 1e-06
MESH = pl.DeviceIdType.MESH
NEG = -1e30
LANES = 128
BF = jnp.bfloat16
F32 = jnp.float32


def pad_up(x, m):
    return (x + m - 1) // m * m


def nn(a, b):
    return jnp.dot(a, b, preferred_element_type=F32)


def nt(a, b):
    return lax.dot_general(a, b, (((1,), (1,)), ((), ())), preferred_element_type=F32)


def tn(a, b):
    return lax.dot_general(a, b, (((0,), (0,)), ((), ())), preferred_element_type=F32)


def bias_kernel(rows, buckets_ref, table_ref, out_ref):
    tables, highs, _ = table_ref.shape
    prow, pcol = buckets_ref.shape
    step = 16

    def body(block, carry):
        at = pl.multiple_of(block * step, step)
        for half in range(pcol // LANES):
            ids = buckets_ref[pl.ds(at, step), half * LANES : (half + 1) * LANES]
            low = ids & (LANES - 1)
            high = lax.shift_right_logical(ids, 7)
            column = lax.broadcasted_iota(jnp.int32, (step, LANES), 1) + half * LANES
            inside = column < rows
            picks = [high == number for number in range(highs)]
            for t in range(tables):
                value = jnp.full((step, LANES), NEG, F32)
                for number in range(highs):
                    row = jnp.broadcast_to(table_ref[t, number : number + 1, :], (step, LANES))
                    got = jnp.take_along_axis(row, low, axis=1)
                    value = jnp.where(picks[number], got, value)
                value = jnp.where(inside, value, NEG)
                out_ref[t, pl.ds(at, step), half * LANES : (half + 1) * LANES] = value.astype(BF)
        return carry

    lax.fori_loop(0, prow // step, body, 0)


def position_bias(buckets, tables, rows):
    return pl.pallas_call(
        functools.partial(bias_kernel, rows),
        out_shape=jax.ShapeDtypeStruct((tables.shape[0],) + buckets.shape, BF),
        in_specs=[pl.BlockSpec(memory_space=pltpu.VMEM)] * 2,
        out_specs=pl.BlockSpec(memory_space=pltpu.VMEM),
        name="position_bias",
        cost_estimate=pl.CostEstimate(flops=10**7, bytes_accessed=10**6, transcendentals=0),
    )(buckets, tables)


def bucket_kernel(rows, highs, buckets_ref, grads_ref, out_ref, acc_ref):
    groups = grads_ref.shape[0]
    pcol = grads_ref.shape[2]
    acc_ref[...] = jnp.zeros_like(acc_ref)
    step = 8

    def body(block, carry):
        at = pl.multiple_of(block * step, step)
        ids_all = buckets_ref[pl.ds(at, step), :]
        grads_all = grads_ref[:, pl.ds(at, step), :]
        total = None
        for r in range(step):
            ids = ids_all[r : r + 1, :]
            low = ids & (LANES - 1)
            high = lax.shift_right_logical(ids, 7)
            spots = lax.broadcasted_iota(jnp.int32, (LANES, pcol), 0)
            hot = jnp.where(spots == low, 1.0, 0.0).astype(BF)
            grads = grads_all[:, r, :]
            parts = [jnp.where(high == number, grads, 0.0) for number in range(highs)]
            left = jnp.concatenate(parts, 0).astype(BF)
            got = nt(left, hot)
            total = got if total is None else total + got
        acc_ref[...] += total
        return carry

    lax.fori_loop(0, pad_up(rows, step) // step, body, 0)
    out_ref[...] = acc_ref[...].reshape(out_ref.shape)


def bucket_sums(buckets, grads, rows, highs):
    groups = grads.shape[0]
    return pl.pallas_call(
        functools.partial(bucket_kernel, rows, highs),
        out_shape=jax.ShapeDtypeStruct((highs, groups, LANES), F32),
        in_specs=[pl.BlockSpec(memory_space=pltpu.VMEM)] * 2,
        out_specs=pl.BlockSpec(memory_space=pltpu.VMEM),
        scratch_shapes=[pltpu.VMEM((highs * groups, LANES), F32)],
        name="bucket_sums",
        compiler_params=pltpu.CompilerParams(vmem_limit_bytes=40 * 2**20),
        cost_estimate=pl.CostEstimate(flops=10**9, bytes_accessed=3 * 10**6, transcendentals=0),
    )(buckets, grads)


class Layout:
    def __init__(self, layers, heads, head, rows, prow, width, hidden):
        self.layers, self.heads, self.head = layers, heads, head
        self.rows, self.prow, self.width, self.hidden = rows, prow, width, hidden
        self.own = heads * head
        self.halves = 2 * layers
        h = self.halves
        self.scale_at, self.bias_at, self.gain_at, self.shift_at = 0, h, 2 * h, 3 * h
        self.qv_at, self.up_at, self.token_at = 4 * h, 4 * h + layers, 4 * h + 2 * layers
        self.smalls = pad_up(4 * h + 2 * layers + 1, 8)


def norm_stats(x):
    mean = jnp.mean(x, -1, keepdims=True)
    centered = x - mean
    r = lax.rsqrt(jnp.mean(centered * centered, -1, keepdims=True) + EPS)
    return centered * r, r


def blocks_kernel(
    lay,
    x0_ref, g4_ref, mask_ref, vec_ref, qvb_ref, upb_ref, bias_ref,
    wqkv_ref, wout_ref, wup_ref, wdn_ref,
    v4_ref, g0_ref, small_ref, ds_ref,
    gqkv_ref, gout_ref, gup_ref, gdn_ref,
    v_buf, normed, branch, qkv, probs, ctx, act, gate, bgrad, dqkv, acc, g_buf,
    core_out, core_in, far_out, far_in,
    core_send, core_recv, far_send, far_recv, row_send, row_recv,
):
    section = lax.axis_index("section")
    mate = {"section": section + 1 - 2 * lax.rem(section, 2)}
    far = {"section": lax.rem(section + 2, 4)}
    halves, prow, width = lay.halves, lay.prow, lay.width
    own, hid, hd = lay.own, lay.hidden, lay.head

    barrier = pltpu.get_barrier_semaphore()
    for other in (mate, far):
        pl.semaphore_signal(barrier, inc=1, device_id=other, device_id_type=MESH)
    pl.semaphore_wait(barrier, 2)

    small_ref[...] = jnp.zeros_like(small_ref)

    def add_small(at, row, columns=slice(None)):
        small_ref[at : at + 1, columns] = row

    def column_sum(x):
        return jnp.sum(x, 0, keepdims=True)

    def vec(kind, k):
        return vec_ref[kind * halves + k : kind * halves + k + 1, :]

    def share_rows(ref, step):
        return pltpu.make_async_remote_copy(
            src_ref=ref.at[0], dst_ref=ref.at[1],
            send_sem=row_send.at[step], recv_sem=row_recv.at[step],
            device_id=mate, device_id_type=MESH,
        )

    def to_mate(step):
        return pltpu.make_async_remote_copy(
            src_ref=core_out.at[step], dst_ref=core_in.at[step],
            send_sem=core_send.at[step], recv_sem=core_recv.at[step],
            device_id=mate, device_id_type=MESH,
        )

    def to_far(step):
        return pltpu.make_async_remote_copy(
            src_ref=far_out.at[step], dst_ref=far_in.at[step],
            send_sem=far_send.at[step], recv_sem=far_recv.at[step],
            device_id=far, device_id_type=MESH,
        )

    def sum_up_start(step):
        to_mate(step).wait_recv()
        far_out[step] = (acc[...] + core_in[step].astype(F32)).astype(BF)
        to_far(step).start()

    def sum_up_end(step):
        to_far(step).wait_recv()
        return far_out[step].astype(F32) + far_in[step].astype(F32)

    def finish_sends(step, ref):
        share_rows(ref, step).wait_send()
        to_mate(step).wait_send()
        to_far(step).wait_send()

    scale = hd ** -0.5

    def attention_page(l, k, slot):
        rows = nn(normed[k, slot], wqkv_ref[l])
        rows = rows + qvb_ref[l : l + 1, :]
        qkv[l, slot] = rows.astype(BF)
        for h in range(lay.heads):
            q = qkv[l, slot, :, h * hd : (h + 1) * hd]
            kk = qkv[l, slot, :, own + h * hd : own + (h + 1) * hd]
            vv = qkv[l, slot, :, 2 * own + h * hd : 2 * own + (h + 1) * hd]
            s = nt(q, kk) * scale + bias_ref[l * lay.heads + h, :, :prow].astype(F32)
            e = jnp.exp(s - jnp.max(s, -1, keepdims=True))
            p = (e / jnp.sum(e, -1, keepdims=True)).astype(BF)
            probs[l, slot, h] = p
            ctx[l, slot, :, h * hd : (h + 1) * hd] = nn(p, vv).astype(BF)
        return nn(ctx[l, slot], wout_ref[l])

    def mlp_page(l, k, slot):
        pre = nn(normed[k, slot], wup_ref[l]) + upb_ref[l : l + 1, :]
        c0, c1 = 0.7978845608028654, 0.044715
        square = pre * pre
        t = jnp.tanh(c0 * (pre + c1 * pre * square))
        act[l, slot] = (0.5 * pre * (1.0 + t)).astype(BF)
        slope = 0.5 * (1.0 + t) + 0.5 * pre * (1.0 - t * t) * (c0 * (1.0 + 3.0 * c1 * square))
        gate[l, slot] = slope.astype(BF)
        return nn(act[l, slot], wdn_ref[l])

    v_buf[0] = x0_ref[...]
    for k in range(halves):
        l = k // 2
        x = v_buf[k].astype(F32)
        xhat, _ = norm_stats(x)
        normed[k, 0] = (xhat * vec(0, k) + vec(1, k)).astype(BF)
        share_rows(normed.at[k], k).start()
        page = attention_page if k % 2 == 0 else mlp_page
        acc[...] = page(l, k, 0)
        share_rows(normed.at[k], k).wait_recv()
        core_out[k] = page(l, k, 1).astype(BF)
        to_mate(k).start()
        sum_up_start(k)
        b = sum_up_end(k) + vec(3, k)
        branch[k] = b
        after = (v_buf[k].astype(F32) + vec(2, k) * b).astype(BF)
        if k + 1 < halves:
            v_buf[k + 1] = after
        else:
            v4_ref[...] = after
        finish_sends(k, normed.at[k])

    g_buf[...] = g4_ref[...].astype(F32)
    for k in reversed(range(halves)):
        l = k // 2
        step = halves + (halves - 1 - k)
        g = g_buf[...]
        add_small(lay.scale_at + k, column_sum(g * branch[k]))
        low = (g * vec(2, k)).astype(BF)
        bgrad[k, 0] = low
        share_rows(bgrad.at[k], step).start()
        add_small(lay.bias_at + k, column_sum(low.astype(F32)))

        def attention_back(slot):
            dctx = nt(bgrad[k, slot], wout_ref[l]).astype(BF)
            for h in range(lay.heads):
                q = qkv[l, slot, :, h * hd : (h + 1) * hd]
                kk = qkv[l, slot, :, own + h * hd : own + (h + 1) * hd]
                vv = qkv[l, slot, :, 2 * own + h * hd : 2 * own + (h + 1) * hd]
                dc = dctx[:, h * hd : (h + 1) * hd]
                low_p = probs[l, slot, h]
                p = low_p.astype(F32)
                dp = nt(dc, vv)
                ds = (p * (dp - jnp.sum(p * dp, -1, keepdims=True))).astype(BF)
                where_ds = (l * lay.heads + h) * 2 + slot
                ds_ref[where_ds, :, :prow] = ds.astype(F32)
                dqkv[slot, :, h * hd : (h + 1) * hd] = (nn(ds, kk) * scale).astype(BF)
                dqkv[slot, :, own + h * hd : own + (h + 1) * hd] = (tn(ds, q) * scale).astype(BF)
                dqkv[slot, :, 2 * own + h * hd : 2 * own + (h + 1) * hd] = tn(low_p, dc).astype(BF)
            return nt(dqkv[slot], wqkv_ref[l])

        def mlp_back(slot):
            dact = nt(bgrad[k, slot], wdn_ref[l])
            dqkv_or = (dact * gate[l, slot].astype(F32)).astype(BF)
            gate[l, slot] = dqkv_or
            return nt(dqkv_or, wup_ref[l])

        page = attention_back if k % 2 == 0 else mlp_back
        acc[...] = page(0)
        share_rows(bgrad.at[k], step).wait_recv()
        core_out[step] = page(1).astype(BF)
        to_mate(step).start()
        sum_up_start(step)

        both = 2 * prow
        bg = bgrad[k].reshape(both, width)
        nm = normed[k].reshape(both, width)
        if k % 2 == 0:
            dall = dqkv[...].reshape(both, 3 * own)
            gout_ref[l] = tn(ctx[l].reshape(both, own), bg).astype(BF)
            gqkv_ref[l] = tn(nm, dall).astype(BF)
            sums = column_sum(dall.astype(F32))
            add_small(lay.qv_at + l, sums[:, :own], slice(0, own))
            add_small(lay.qv_at + l, sums[:, 2 * own :], slice(2 * LANES, 2 * LANES + own))
        else:
            dpre = gate[l].reshape(both, hid)
            gdn_ref[l] = tn(act[l].reshape(both, hid), bg).astype(BF)
            gup_ref[l] = tn(nm, dpre).astype(BF)
            add_small(lay.up_at + l, column_sum(dpre.astype(F32)))

        ng = sum_up_end(step)
        xhat, r = norm_stats(v_buf[k].astype(F32))
        add_small(lay.gain_at + k, column_sum(ng * xhat))
        add_small(lay.shift_at + k, column_sum(ng))
        t = ng * vec(0, k)
        inner = t - jnp.mean(t, -1, keepdims=True) - xhat * jnp.mean(t * xhat, -1, keepdims=True)
        g = g_buf[...] + r * inner
        if k > 0:
            g_buf[...] = g.astype(BF).astype(F32)
        else:
            g0_ref[...] = g * (1.0 - mask_ref[...])
            add_small(lay.token_at, column_sum(g * mask_ref[...]))
        finish_sends(step, bgrad.at[k])


def run_blocks(lay, *operands):
    L, prow, width, own, hid = lay.layers, lay.prow, lay.width, lay.own, lay.hidden
    halves, steps = lay.halves, 2 * lay.halves
    pcol = operands[6].shape[2]
    shape = jax.ShapeDtypeStruct
    rows = (prow, width)
    return pl.pallas_call(
        functools.partial(blocks_kernel, lay),
        out_shape=(
            shape(rows, BF), shape(rows, F32), shape((lay.smalls, width), F32),
            shape((2 * L * lay.heads, prow, pcol), F32),
            shape((L, width, 3 * own), BF), shape((L, own, width), BF),
            shape((L, width, hid), BF), shape((L, hid, width), BF),
        ),
        in_specs=[pl.BlockSpec(memory_space=pltpu.VMEM)] * 11,
        out_specs=[pl.BlockSpec(memory_space=pltpu.VMEM)] * 8,
        scratch_shapes=[
            pltpu.VMEM((halves,) + rows, BF),
            pltpu.VMEM((halves, 2) + rows, BF),
            pltpu.VMEM((halves,) + rows, F32),
            pltpu.VMEM((L, 2, prow, 3 * own), BF),
            pltpu.VMEM((L, 2, lay.heads, prow, prow), BF),
            pltpu.VMEM((L, 2, prow, own), BF),
            pltpu.VMEM((L, 2, prow, hid), BF),
            pltpu.VMEM((L, 2, prow, hid), BF),
            pltpu.VMEM((halves, 2) + rows, BF),
            pltpu.VMEM((2, prow, 3 * own), BF),
            pltpu.VMEM(rows, F32),
            pltpu.VMEM(rows, F32),
            pltpu.VMEM((steps,) + rows, BF),
            pltpu.VMEM((steps,) + rows, BF),
            pltpu.VMEM((steps,) + rows, BF),
            pltpu.VMEM((steps,) + rows, BF),
        ] + [pltpu.SemaphoreType.DMA((steps,))] * 6,
        compiler_params=pltpu.CompilerParams(
            collective_id=1, has_side_effects=True, vmem_limit_bytes=60 * 2**20
        ),
        name="blocks",
        cost_estimate=pl.CostEstimate(flops=9 * 10**9, bytes_accessed=2 * 10**7, transcendentals=10**7),
    )(*operands)


def per_device(
    patches, page_mask, mask_token, buckets, ln_gain, ln_shift, layer_scale, branch_bias,
    qkv_weight, qv_bias, out_weight, rel_table, up_weight, up_bias, down_weight, cotangent,
):
    section = lax.axis_index("section")
    sections = lax.axis_size("section")
    dp = lax.axis_index("dp")
    ranks = lax.axis_size("dp")
    core = lax.rem(section, 2)
    layers = qkv_weight.shape[0]
    pages, rows, width = patches.shape
    all_heads = rel_table.shape[1]
    bucket_count = rel_table.shape[2]
    head = width // all_heads
    heads = all_heads // sections
    own = heads * head
    hidden = up_weight.shape[2]
    hid = hidden // sections
    prow, pcol = pad_up(rows, 16), pad_up(rows, LANES)
    highs = pad_up(bucket_count, LANES) // LANES
    lay = Layout(layers, heads, head, rows, prow, width, hid)
    halves = 2 * layers

    unit = down_weight.shape[1] // sections
    shard = qkv_weight.shape[1]

    def pick(x, axis):
        return lax.dynamic_index_in_dim(x, section, axis, keepdims=False)

    qkv_own = pick(qkv_weight.reshape(layers, shard, 3, sections, own), 3).reshape(layers, shard, 3 * own)
    up_own = pick(up_weight.reshape(layers, shard, ranks, sections, unit), 3).reshape(layers, shard, hid)
    dn_own = pick(down_weight.reshape(layers, sections, unit, width), 1)

    def gathered(x):
        return lax.all_gather(x, "dp", axis=1, tiled=True)

    wqkv, wup, wdn = gathered(qkv_own), gathered(up_own), gathered(dn_own)
    wout = pick(gathered(out_weight).reshape(layers, sections, own, width), 1)

    vecs = jnp.concatenate([ln_gain, ln_shift, layer_scale, branch_bias], 0)
    vecs = lax.all_gather(vecs, "section", axis=1, tiled=False).reshape(4 * halves, width).astype(F32)
    qv_own = pick(qv_bias.reshape(layers, 2, sections, own), 2).astype(F32)
    qv_vec = jnp.concatenate([qv_own[:, 0], jnp.zeros_like(qv_own[:, 0]), qv_own[:, 1]], 1)
    upb_own = pick(up_bias.reshape(layers, ranks, sections, unit), 2).reshape(layers, hid).astype(F32)

    tables = pick(rel_table.reshape(layers, sections, heads, bucket_count), 1).astype(F32)
    tables = jnp.pad(tables, ((0, 0), (0, 0), (0, highs * LANES - bucket_count)))
    tables = tables.reshape(layers * heads, highs, LANES)
    ids = jnp.pad(buckets, ((0, prow - rows), (0, pcol - rows)))
    bias = position_bias(ids, tables, rows)

    def page_of(x):
        return lax.dynamic_index_in_dim(x, core, 0, keepdims=False)

    mask_own = page_of(page_mask)[:, None]
    x0 = jnp.where(mask_own == 1, mask_token, page_of(patches))
    x0 = jnp.pad(x0, ((0, prow - rows), (0, 0)))
    g4 = jnp.pad(page_of(cotangent), ((0, prow - rows), (0, 0)))
    mask_f = jnp.pad((mask_own == 1).astype(F32), ((0, prow - rows), (0, 0)))

    v4, g0, small, ds, gqkv, gout, gup, gdn = run_blocks(
        lay, x0, g4, mask_f, vecs, qv_vec, upb_own, bias, wqkv, wout, wup, wdn
    )

    def scattered(x):
        return lax.psum_scatter(x, "dp", scatter_dimension=1, tiled=True)

    sqkv, sup, sdn = scattered(gqkv), scattered(gup), scattered(gdn)

    def everywhere(x, axis):
        return lax.all_gather(x, "section", axis=axis, tiled=False)

    qkv_all = everywhere(sqkv.reshape(layers, shard, 3, own), 3).reshape(layers, shard, 3 * width)
    qkv_cols = 3 * width // sections
    qkv_out = lax.dynamic_slice_in_dim(qkv_all, section * qkv_cols, qkv_cols, 2).astype(F32)
    up_all = everywhere(sup.reshape(layers, shard, ranks, unit), 3).reshape(layers, shard, hidden)
    up_out = lax.dynamic_slice_in_dim(up_all, section * hid, hid, 2).astype(F32)
    cols = width // sections
    dn_all = lax.all_to_all(
        sdn.reshape(layers, unit, sections, cols), "section", split_axis=2, concat_axis=1, tiled=False
    )
    dn_out = dn_all.reshape(layers, sections * unit, cols).astype(F32)
    out_full = everywhere(gout, 1).reshape(layers, width, width)
    out_mine = lax.psum_scatter(out_full, "dp", scatter_dimension=1, tiled=True)
    out_out = lax.dynamic_slice_in_dim(out_mine, section * cols, cols, 2).astype(F32)

    def pages_of(x):
        both = lax.all_gather(x[:rows], "section", axis=0, tiled=False)[:pages]
        return lax.dynamic_slice_in_dim(both, section * cols, cols, 2)

    block_out = pages_of(v4)
    input_out = pages_of(g0)

    sums = bucket_sums(ids, ds, rows, highs)
    sums = sums.reshape(highs, layers, heads, 2, LANES).sum(3)
    table_own = sums.transpose(1, 2, 0, 3).reshape(layers, heads, highs * LANES)[:, :, :bucket_count]

    once = (section < 2).astype(F32)
    replicated = small[: 4 * halves] * once
    token = small[lay.token_at] * once
    qv_rows = small[lay.qv_at : lay.qv_at + layers]
    qv_pair = jnp.stack([qv_rows[:, :own], qv_rows[:, 2 * LANES : 2 * LANES + own]], 1)
    here = (jnp.arange(sections) == section).astype(F32)
    qv_full = (qv_pair[:, :, None, :] * here[None, None, :, None]).reshape(layers, 2 * width)
    up_rows = small[lay.up_at : lay.up_at + layers].reshape(layers, ranks, 1, unit)
    up_full = (up_rows * here[None, None, :, None]).reshape(layers, hidden)
    table_full = (table_own[:, None] * here[None, :, None, None]).reshape(layers, all_heads, bucket_count)
    replicated, token, qv_total, up_total, table_total = lax.psum(
        (replicated, token, qv_full, up_full, table_full), ("section", "dp")
    )

    def own_row(at):
        return lax.dynamic_slice_in_dim(replicated, at + section, 1, 0)

    return (
        block_out, input_out, qkv_out, out_out, up_out, dn_out,
        qv_total, up_total, table_total,
        own_row(lay.gain_at), own_row(lay.shift_at), own_row(lay.scale_at), own_row(lay.bias_at),
        token,
    )


def solution(mesh):
    rows3 = P("dp", None, None)
    part = P("section", None)
    weight = P(None, "dp", None)
    in_specs = (
        rows3, P("dp", None), P(), P(), part, part, part, part,
        weight, P(), weight, P(), weight, P(), weight, rows3,
    )
    cut = P("dp", None, "section")
    grad = P(None, "dp", "section")
    out_specs = (cut, cut, grad, grad, grad, grad, P(), P(), P(), part, part, part, part, P())
    return jax.shard_map(per_device, mesh=mesh, in_specs=in_specs, out_specs=out_specs, check_vma=False)
```

time: 1510 us -> 986 us (0.65)
  other arithmetic: 324 us -> 9.16 us
  local copies, waits for them, and re-layouts: 317 us -> 50.6 us
  Pallas kernels: 0 us -> 132 us
  waiting for transfers between devices: 631 us -> 749 us
  matrix products: 72.3 us -> 0 us
  loops' own time: 60.9 us -> 0 us
  blocking collectives: 47.4 us -> 17 us
  starting transfers between devices: 33 us -> 4.02 us
    all_gather x2 -> x8, waiting for transfers between devices: 9.21 us -> 257 us  [the longest x4 178 us: gathered(): return lax.all_gather(x, 'dp', axis=1, tiled=True)]
    scatter-add x1 -> x0, other arithmetic: 208 us -> none  [per_device(): jax.ops.segment_sum(table_pairs, buckets.reshape(-1), num_segments=bucket...]
    ppermute x8 -> x0, waiting for transfers between devices: 198 us -> none  [passed_along(): lax.ppermute(value, axis, [(source, source + steps) for source in range(i...]
    gather x3 -> x0, local copies, waits for them, and re-layouts: 142 us -> none  [per_device(): position_bias = jnp.take(table_now, buckets, axis=1)]
    pallas_call x0 -> x3, Pallas kernels: none -> 132 us  [the longest x1 118 us: run_blocks(): pl.pallas_call(functools.partial(blocks_kernel, lay), out_shape=(shape(ro...]
    psum x2, waiting for transfers between devices: 123 us -> 239 us  [per_device(): lax.psum((replicated, token, qv_full, up_full, table_full), ('section', '...]
    unnamed x14, waiting for transfers between devices: 81.2 us -> 2.58 us
    dot_general x32 -> x0, matrix products: 72.3 us -> none  [the longest x4 16.2 us: attention_parts(): jnp.einsum('phij,pjhd->pihd', probs_low, value_heads, preferred_element_t...]
  transfers between devices with their start and end apart: 19 -> 15, of which waited for: 15 -> 14; matrix products, arithmetic and copies ran while one was open for 30% -> 5% of each run, Pallas kernels for 0% -> 1%
where the time goes in v1:
time: 986 us; the launch traced here: 977 us
  waiting for transfers between devices  749 us (76%)
  Pallas kernels  132 us (13%)
  local copies, waits for them, and re-layouts  50.6 us (5%)
  blocking collectives  17 us (2%)
  between operations  14.9 us (2%)
    psum x2, waiting for transfers between devices, per_device(): lax.psum((replicated, token, qv_full, up_full, table_full), ('section', '...  239 us
    reduce_scatter x3, waiting for transfers between devices, scattered(): return lax.psum_scatter(x, 'dp', scatter_dimension=1, tiled=True)  185 us
    all_gather x4, waiting for transfers between devices, gathered(): return lax.all_gather(x, 'dp', axis=1, tiled=True)  178 us
    pallas_call x1, Pallas kernels, run_blocks(): pl.pallas_call(functools.partial(blocks_kernel, lay), out_shape=(shape(ro...  118 us
    reduce_scatter x1, waiting for transfers between devices, per_device(): out_mine = lax.psum_scatter(out_full, 'dp', scatter_dimension=1, tiled=True)  64.9 us
    all_gather x2, waiting for transfers between devices, pages_of(): both = lax.all_gather(x[:rows], 'section', axis=0, tiled=False)[:pages]  41.2 us
    all_gather x2, waiting for transfers between devices, everywhere(): return lax.all_gather(x, 'section', axis=axis, tiled=False)  38.2 us
  transfers between devices with their start and end apart: 15, of which 14 were waited for; matrix products, arithmetic and copies ran while one was open for 5% of the time, Pallas kernels for 1%

profile of v1, /device:TPU:0, one launch (start us, length us, event | category | flops | bytes accessed | tf_op | source)
XLA Modules:
  0.0 977.4 jit_solution(5180678232328334339)
XLA Ops:
  8.0 2.9 reshape.149
  12.0 0.9 copy.102
  12.9 3.5 reshape.152
  16.4 2.5 dynamic-slice_reduce_fusion
  19.0 1.0 reshape.153
  20.9 1.3 constant_dynamic-slice_fusion.10
  22.5 0.7 pad.22.x0_ref
  27.1 6.2 all-gather
  34.1 4.5 position_bias.1.bias_ref
  39.8 25.2 %all-gather.18.cloned.1.call-done = bf16[2,768,768]{2,1,0:T(8,128)(2,1)} async-done(((bf16[2,96,768]{2,1,0:T(8,128)(2,1)}), bf16[2,768,768]{2,1,0:T(8,128)(2,1)}) %all-gather.18.cloned.1.call-update) | async-done | bytes 2359312 | tf_op jit(solution)/shard_map/all_gather | solution.py:399
  65.0 1.9 dynamic-slice_bitcast_fusion.wout_ref
  67.0 46.4 %all-gather.16.cloned.1.call-done.wqkv_ref = bf16[2,768,576]{2,1,0:T(8,128)(2,1)} async-done(((bf16[2,96,576]{2,1,0:T(8,128)(2,1)}), bf16[2,768,576]{2,1,0:T(8,128)(2,1)}) %all-gather.16.cloned.1.call-update) | async-done | bytes 1769488 | tf_op jit(solution)/shard_map/all_gather | solution.py:399
  113.3 53.8 %all-gather.20.cloned.1.call-done.wup_ref = bf16[2,768,768]{2,1,0:T(8,128)(2,1)} async-done(((bf16[2,96,768]{2,1,0:T(8,128)(2,1)}), bf16[2,768,768]{2,1,0:T(8,128)(2,1)}) %all-gather.20.cloned.1.call-update) | async-done | bytes 2359312 | tf_op jit(solution)/shard_map/all_gather | solution.py:399
  167.1 52.5 %all-gather.24.cloned.1.call-done = bf16[2,1,768,768]{3,2,0,1:T(8,128)(2,1)} async-done(((bf16[2,1,96,768]{3,2,0,1:T(8,128)(2,1)}), bf16[2,1,768,768]{3,2,0,1:T(8,128)(2,1)}) %all-gather.24.cloned.1.call-update) | async-done | bytes 2359312 | tf_op jit(solution)/shard_map/all_gather | solution.py:399
  219.7 118.2 %blocks.1 = (bf16[208,768]{1,0:T(8,128)(2,1)}, f32[208,768]{1,0:T(8,128)}, f32[24,768]{1,0:T(8,128)}, f32[12,208,256]{2,1,0:T(8,128)}, bf16[2,768,576]{2,1,0:T(8...) custom-call(bf16[208,768]{1,0:T(8,128)(2,1)} %pad.22.x0_ref, ...), custom_call_target="tpu_custom_call" | custom-call | flops 8999999488 | bytes 20000000 | tf_op jit(solution)/shard_map/blocks/pallas_call | solution.py:329
  344.3 0.9 slice_bitcast_fusion
  345.3 59.4 %reduce-scatter.9.cloned.1.call-done = bf16[2,96,768]{2,1,0:T(8,128)(2,1)} async-done(((bf16[2,768,768]{2,1,0:T(8,128)(2,1)}), bf16[2,96,768]{2,1,0:T(8,128)(2,1)}) %reduce-scatter.9.cloned.1.call-update) | async-done | bytes 294928 | tf_op jit(solution)/shard_map/reduce_scatter | solution.py:430
  404.6 2.2 all_gather_reshape.7
  406.9 22.3 %all-gather.26.cloned.1.call-done = bf16[2,768,768]{2,1,0:T(8,128)(2,1)} async-done(((bf16[2,192,768]{2,1,0:T(8,128)(2,1)}), bf16[2,768,768]{2,1,0:T(8,128)(2,1)}) %all-gather.26.cloned.1.call-update) | async-done | bytes 2359312 | tf_op jit(solution)/shard_map/all_gather | solution.py:435
  429.4 1.7 copy-done.2
  431.2 9.7 bucket_sums.1
  441.8 116.5 %all-reduce.11.cloned.1.call-done = (f32[2,1536]{1,0:T(2,128)}, f32[2,3072]{1,0:T(2,128)}, f32[16,768]{1,0:T(8,128)}, f32[768]{0:T(1024)}) async-done(((f32[2,1536]{1,0:T(2,128)}, f32[2,3072]{1,0:T(2,128)}, f32[16,768]{1,0:T(8,128)}, f32[768]{0:T(1024)}), (f32[2,1536]{1,0:T(2,128)}, f32[2,3072]{1,0:T(2,128)}, f32[16,768]{1,0:T(8,128)}, f32[768]{0:T(1024)})) %all-reduce.11.cloned.1.call-update) | async-done | bytes 89104 | tf_op jit(solution)/shard_map/psum | solution.py:472
  558.3 1.4 constant_dynamic-slice_fusion
  559.7 20.0 %all-gather.28.cloned.1.call-done = bf16[4,197,768]{2,1,0:T(8,128)(2,1)} async-done(((bf16[1,197,768]{2,1,0:T(8,128)(2,1)}), bf16[4,197,768]{2,1,0:T(8,128)(2,1)}) %all-gather.28.cloned.1.call-update) | async-done | bytes 1210384 | tf_op jit(solution)/shard_map/all_gather | solution.py:452
  579.7 1.1 slice.57
  581.0 0.8 copy.114
  581.8 68.3 %reduce-scatter.5.cloned.1.call-done = bf16[2,96,576]{2,1,0:T(8,128)(2,1)} async-done(((bf16[2,768,576]{2,1,0:T(8,128)(2,1)}), bf16[2,96,576]{2,1,0:T(8,128)(2,1)}) %reduce-scatter.5.cloned.1.call-update) | async-done | bytes 221200 | tf_op jit(solution)/shard_map/reduce_scatter | solution.py:430
  650.1 1.1 copy.106
  651.4 10.7 %all_gather.52 = bf16[2,96,3,4,192]{4,1,2,0,3:T(8,128)(2,1)S(1)} all-gather(bf16[2,96,3,1,192]{4,1,2,0,3:T(8,128)(2,1)S(1)} %copy.107), channel_id=1, replica_groups=mesh['section'=4,'dp'=8] {'section'}, dimensions={3}, use_global_device_ids=true | all-gather | bytes 1105920 | tf_op jit(solution)/shard_map/all_gather | solution.py:435
  662.1 0.9 copy.108
  663.1 1.1 reshape.155
  664.2 57.8 %reduce-scatter.11.cloned.1.call-done = bf16[2,96,768]{2,1,0:T(8,128)(2,1)} async-done(((bf16[2,768,768]{2,1,0:T(8,128)(2,1)}), bf16[2,96,768]{2,1,0:T(8,128)(2,1)}) %reduce-scatter.11.cloned.1.call-update) | async-done | bytes 294928 | tf_op jit(solution)/shard_map/reduce_scatter | solution.py:430
  721.9 1.3 broadcast_in_dim_reshape.3
  723.3 0.8 copy.110
  724.1 3.5 all-to-all-start
  727.5 0.9 dynamic-slice_convert_fusion.1
  728.4 21.2 %all-gather.30.cloned.1.call-done = f32[4,197,768]{2,1,0:T(8,128)} async-done(((f32[1,197,768]{2,1,0:T(8,128)}), f32[4,197,768]{2,1,0:T(8,128)}) %all-gather.30.cloned.1.call-update) | async-done | bytes 2420752 | tf_op jit(solution)/shard_map/all_gather | solution.py:452
  749.6 1.3 slice-done
  751.1 0.9 copy.115
  752.5 1.2 reshape.165
  753.7 15.9 %all-gather.22.cloned.1.call-done = bf16[2,96,8,4,96]{4,2,1,0,3:T(8,128)(2,1)} async-done(((bf16[2,96,8,1,96]{4,2,1,0,3:T(8,128)(2,1)}), bf16[2,96,8,4,96]{4,2,1,0,3:T(8,128)(2,1)}) %all-gather.22.cloned.1.call-update) | async-done | bytes 1179664 | tf_op jit(solution)/shard_map/all_gather | solution.py:435
  769.6 3.4 copy.109
  773.0 3.0 reshape.157
  776.0 1.8 dynamic-slice_convert_fusion
  777.8 64.9 %reduce-scatter.7.cloned.1.call-done = bf16[2,96,768]{2,1,0:T(8,128)(2,1)} async-done(((bf16[2,768,768]{2,1,0:T(8,128)(2,1)}), bf16[2,96,768]{2,1,0:T(8,128)(2,1)}) %reduce-scatter.7.cloned.1.call-update) | async-done | bytes 294928 | tf_op jit(solution)/shard_map/reduce_scatter | solution.py:448
  842.7 1.7 dynamic-slice_convert_fusion.2
  844.4 122.7 %all-reduce.9.cloned.1.call-done = f32[2,12,732]{2,0,1:T(2,128)} async-done(((f32[2,12,732]{2,0,1:T(2,128)}), f32[2,12,732]{2,0,1:T(2,128)}) %all-reduce.9.cloned.1.call-update) | async-done | bytes 70288 | tf_op jit(solution)/shard_map/psum | solution.py:472
  968.3 1.5 copy.142
  (130 shorter events, 19.0 us)
Async XLA Ops:
  7.2 12.9 %copy-start = (bf16[2,384,768]{2,1,0:T(8,128)(2,1)S(1)}, bf16[2,384,768]{2,1,0:T(8,128)(2,1)}, u32[]{:S(2)}) copy-start(bf16[2,384,768]{2,1,0:T(8,128)(2,1)} %param.30) | copy-start | bytes 3538948
  7.2 57.8 %all-gather.18.cloned.1.call-start = ((), (), s32[]{:S(2)}) async-start(), calls=%async_computation.6 | async-start | bytes 2654208 | tf_op jit(solution)/shard_map/all_gather | solution.py:399
  7.9 105.4 %all-gather.16.cloned.1.call-start = ((), (), s32[]{:S(2)}) async-start(), calls=%async_computation.5 | async-start | bytes 2211840 | tf_op jit(solution)/shard_map/all_gather | solution.py:399
  12.8 154.3 %all-gather.20.cloned.1.call-start = ((), (), s32[]{:S(2)}) async-start(), calls=%async_computation.7 | async-start | bytes 2654208 | tf_op jit(solution)/shard_map/all_gather | solution.py:399
  18.9 2.0 copy-start.3
  18.9 2.0 copy-start.4
  20.0 199.7 %all-gather.24.cloned.1.call-start = ((), (), s32[]{:S(2)}) async-start(), calls=%async_computation.14 | async-start | bytes 2654208 | tf_op jit(solution)/shard_map/all_gather | solution.py:399
  20.8 383.8 %reduce-scatter.9.cloned.1.call-start = ((), (), s32[]{:S(2)}) async-start(), calls=%async_computation.10 | async-start | bytes 2654208 | tf_op jit(solution)/shard_map/reduce_scatter | solution.py:430
  20.9 1.4 copy-start.19
  20.9 1.4 copy-start.18
  22.2 1.9 copy-start.12
  22.2 3.4 copy-start.7
  22.3 4.0 copy-start.10
  22.3 4.8 copy-start.14
  22.3 4.8 copy-start.15
  22.3 4.8 copy-start.16
  22.3 4.8 copy-start.17
  337.8 1.0 copy-start.8
  337.9 3.9 copy-start.6
  337.9 91.3 %all-gather.26.cloned.1.call-start = ((), (), s32[]{:S(2)}) async-start(), calls=%async_computation.15 | async-start | bytes 2949120 | tf_op jit(solution)/shard_map/all_gather | solution.py:435
  338.5 219.8 %all-reduce.11.cloned.1.call-start = ((), (), s32[]{:S(2)}) async-start(), calls=%async_computation.18 | async-start | bytes 180224 | tf_op jit(solution)/shard_map/psum | solution.py:472
  341.7 238.0 %all-gather.28.cloned.1.call-start = ((), (), s32[]{:S(2)}) async-start(), calls=%async_computation.16 | async-start | bytes 1536000 | tf_op jit(solution)/shard_map/all_gather | solution.py:452
  342.5 307.6 %reduce-scatter.5.cloned.1.call-start = ((), (), s32[]{:S(2)}) async-start(), calls=%async_computation.8 | async-start | bytes 2211840 | tf_op jit(solution)/shard_map/reduce_scatter | solution.py:430
  343.2 1.1 copy-start.5
  343.2 378.7 %reduce-scatter.11.cloned.1.call-start = ((), (), s32[]{:S(2)}) async-start(), calls=%async_computation.12 | async-start | bytes 2654208 | tf_op jit(solution)/shard_map/reduce_scatter | solution.py:430
  343.8 405.8 %all-gather.30.cloned.1.call-start = ((), (), s32[]{:S(2)}) async-start(), calls=%async_computation.17 | async-start | bytes 3072000 | tf_op jit(solution)/shard_map/all_gather | solution.py:452
  345.2 424.3 %all-gather.22.cloned.1.call-start = ((), (), s32[]{:S(2)}) async-start(), calls=%async_computation.11 | async-start | bytes 1966080 | tf_op jit(solution)/shard_map/all_gather | solution.py:435
  406.8 22.6 %copy-start.1 = (s32[208,256]{1,0:T(8,128)S(1)}, s32[208,256]{1,0:T(8,128)}, u32[]{:S(2)}) copy-start(s32[208,256]{1,0:T(8,128)} %pad.26.buckets_ref) | copy-start | bytes 638980
  406.8 435.9 %reduce-scatter.7.cloned.1.call-start = ((), (), s32[]{:S(2)}) async-start(), calls=%async_computation.9 | async-start | bytes 2654208 | tf_op jit(solution)/shard_map/reduce_scatter | solution.py:448
  429.2 537.8 %all-reduce.9.cloned.1.call-start = ((), (), s32[]{:S(2)}) async-start(), calls=%async_computation.13 | async-start | bytes 147456 | tf_op jit(solution)/shard_map/psum | solution.py:472
  429.4 1.7 copy-start.2
  724.1 28.0 %all-to-all-start = ((bf16[2,1,96,4,192]{4,2,0,1,3:T(8,128)(2,1)}), bf16[2,1,96,4,192]{4,2,0,1,3:T(8,128)(2,1)S(1)}, u32[]{:S(2)}, u32[]{:S(2)}) async-start(bf16[2,1,96,4,192]{4,2,0,1,3:T(8,128)(2,1)} %copy.110), calls=%async_computation.4 | async-start | bytes 786432 | tf_op jit(solution)/shard_map/all_to_all | solution.py:443
  749.6 1.3 slice-start
  773.0 194.1 %copy-start.11 = (f32[2,1536]{1,0:T(2,128)S(1)}, f32[2,1536]{1,0:T(2,128)}, u32[]{:S(2)}) copy-start(f32[2,1536]{1,0:T(2,128)} %get-tuple-element.122) | copy-start | bytes 36868
  773.0 194.7 %copy-start.9 = (f32[2,3072]{1,0:T(2,128)S(1)}, f32[2,3072]{1,0:T(2,128)}, u32[]{:S(2)}) copy-start(f32[2,3072]{1,0:T(2,128)} %get-tuple-element.123) | copy-start | bytes 73732
  773.0 196.8 %copy-start.13 = (f32[768]{0:T(1024)S(1)}, f32[768]{0:T(1024)}, u32[]{:S(2)}) copy-start(f32[768]{0:T(1024)} %get-tuple-element.129) | copy-start | bytes 9220
Sparse Core Ops, SparseCore 0:
  10.2 54.7 all-gather.17
  67.2 46.0 all-gather.15
  116.1 51.0 all-gather.19
  169.2 50.4 all-gather.23
  338.0 66.5 reduce-scatter.8
  406.1 23.1 all-gather.25
  436.5 121.6 all-reduce.10
  560.4 19.2 all-gather.27
  583.2 66.8 reduce-scatter.4
  653.8 68.0 reduce-scatter.10
  723.6 26.0 all-gather.29
  751.7 17.8 all-gather.21
  773.5 69.1 reduce-scatter.6
  849.6 117.3 all-reduce.8
